TPU v7x, 32 devices: a whole 2x2x4 slice. The times are simulated.
32 devices in a mesh: slab: 8 (over z, core), dom: 4 (over y, x).
Axes of the slice: x: 2, y: 2, z: 4, core: 2. Of those that a mesh axis runs over, the one named last changes fastest.
Arguments:
- positions: float32 [3, 16384], P(None, ('slab', 'dom')), may hold values from -0.5 to 32.5, as said below
- burgers: float32 [3, 16384], P(None, ('slab', 'dom')), may hold values from -6 to 6
- mobility: float32 [16384], P(('slab', 'dom')), may hold values from 0.5 to 2
- block_cells: int32 [128], P(('slab', 'dom')), may hold values from 0 to 127, as said below
- pairs: int32 [2048, 2], P(('slab', 'dom')), may hold values from 0 to 127, as said below
- pair_count: int32 [32], P(('slab', 'dom')), may hold values from 8 to 64, as said below
Outputs:
- moved: float32 [3, 16384], P(None, ('slab', 'dom'))
- velocity: float32 [3, 16384], P(None, ('slab', 'dom'))
Inputs may be any that keep to these rules, and one draw needn't show every extreme that they name: `block_cells`: block k lies in slab k // (4 * 4) and its cell is 16 times that slab plus 0 to 15. `positions`: each segment lies within 2.5 of its block's cell centre along x and within 1.5 along y and z. `pairs`: device d = s * 4 + e owns blocks d * 4 to (d + 1) * 4 - 1. In device d's slots the first block is one of its own; the second is owned by a device of slab s - 1, s or s + 1 at dom position e - 1, e or e + 1, and differs from the first. Every slot holds such a pair, used or not. `pair_count`: in each slab exactly one device has 64 used slots; the others have at most 32.
All inputs are finite; a program needn't handle non-finite values.
Results may differ from a plain program's by a relative error of at most 0.0003.
Values sent between devices are 32-bit elements; how exact they have to be, the bound alone decides.
No kernel may reach another device: no remote copies, remote signals or barrier semaphores. Data moves between devices by JAX's collectives and lax.ppermute only.
A program may use at most 64 MiB of HBM per device.

v0:
```python
import math
import jax
import jax.numpy as jnp
from jax import lax
from jax.sharding import PartitionSpec as P

BLOCK_SEGS = 128
core_near = 0.25
core_far = 9.0
time_increment = 0.25
pair_batch = 4
hi_prec = lax.Precision.HIGHEST


def padded(x, sides, width):
    for axis, dim in sides:
        peers, length = (lax.axis_size(axis), x.shape[dim])
        up = [(i, (i + 1) % peers) for i in range(peers - 1)]
        down = [(j, i) for i, j in up]
        last = lax.slice_in_dim(x, length - width, length, axis=dim)
        initial = lax.slice_in_dim(x, 0, width, axis=dim)
        before = lax.ppermute(last, axis, up)
        after = lax.ppermute(initial, axis, down)
        x = jnp.concatenate([before, x, after], axis=dim)
    return x


def shifted(block, axis, distance):
    devices = range(lax.axis_size(axis))
    route = [(i - distance, i) for i in devices if i - distance in devices]
    return lax.ppermute(block, axis, route)


def centers(cells):
    slabs = cells // 16
    rest = cells % 16
    return jnp.stack([4 * slabs + 2, 2 * (rest // 4) + 1, 2 * (rest % 4) + 1]).astype(jnp.float32)


def block_moments(posit, burg, cells, ncells, width, base_cell):
    nblk = cells.shape[0]
    offset = posit.reshape(3, nblk, width) - centers(cells)[:, :, None]
    vec = burg.reshape(3, nblk, width)
    first = (vec[:, None] * offset[None]).reshape(9, nblk, width)
    second = (vec[:, None, None] * offset[None, :, None] * offset[None, None, :]).reshape(
        27, nblk, width
    )
    rows = jnp.sum(jnp.concatenate([vec, first, second], axis=0), axis=2)
    onehot = ((cells - base_cell)[:, None] == jnp.arange(ncells, dtype=jnp.int32)[None, :]).astype(
        jnp.float32
    )
    return jnp.dot(rows, onehot, precision=hi_prec)


def far_field(posit, burg, moments):
    ncells = moments.shape[1]
    nblk = ncells // 64
    zeds = centers(jnp.arange(ncells, dtype=jnp.int32)).reshape(3, nblk, 64).transpose(1, 0, 2)
    mblk = moments.reshape(39, nblk, 64).transpose(1, 0, 2)

    def visit(acc, item):
        zpart, mpart = item
        r = posit[:, None, :] - zpart[:, :, None]
        sq = r[0] * r[0] + r[1] * r[1] + r[2] * r[2] + core_far
        inv3 = 1.0 / (sq * jnp.sqrt(sq))
        inv5 = inv3 / sq
        inv7 = inv5 / sq
        qzero = jnp.einsum("kc,kn->cn", mpart[0:3], burg, precision=hi_prec)
        qone = jnp.einsum("kac,kn->acn", mpart[3:12].reshape(3, 3, 64), burg, precision=hi_prec)
        qtwo = jnp.einsum(
            "kabc,kn->abcn", mpart[12:39].reshape(3, 3, 3, 64), burg, precision=hi_prec
        )
        qone_r = jnp.sum(qone * r, axis=0)
        qtwo_r = jnp.sum(qtwo * r[None], axis=1)
        rqr = jnp.sum(r * qtwo_r, axis=0)
        trace = qtwo[0, 0] + qtwo[1, 1] + qtwo[2, 2]
        scal = qzero * inv3 + 3.0 * qone_r * inv5 - 1.5 * trace * inv5 + 7.5 * rqr * inv7
        force = r * scal[None] - qone * inv3[None] - 3.0 * qtwo_r * inv5[None]
        return (acc + jnp.sum(force, axis=1), None)

    start = jnp.zeros(posit.shape, jnp.float32)
    total, unused = lax.scan(visit, start, (zeds, mblk))
    return total


def pair_forces(pos_a, bur_a, pos_b, bur_b, weight):
    r = pos_a[:, :, :, None] - pos_b[:, :, None, :]
    sq = r[0] * r[0] + r[1] * r[1] + r[2] * r[2]
    near_s = sq + core_near
    far_s = sq + core_far
    kern = 1.0 / (near_s * jnp.sqrt(near_s)) - 1.0 / (far_s * jnp.sqrt(far_s))
    coef = jnp.sum(bur_a[:, :, :, None] * bur_b[:, :, None, :], axis=0)
    wgt = weight[:, None, None] * coef * kern
    wr = wgt[None] * r
    return (jnp.sum(wr, axis=3), -jnp.sum(wr, axis=2))


def around_all(stacked):
    grown = padded(stacked[:, None, None, :], (("slab", 1), ("dom", 2)), 1)
    return grown.reshape(stacked.shape[0], -1)


def give_around(window_force, per_dev):
    grid = window_force.reshape(3, 3, 3, per_dev)
    from_above = shifted(grid[:, 0], "slab", -1)
    from_below = shifted(grid[:, 2], "slab", 1)
    row = grid[:, 1] + from_above + from_below
    from_right = shifted(row[:, 0], "dom", -1)
    from_left = shifted(row[:, 2], "dom", 1)
    return row[:, 1] + from_right + from_left


def body(positions, burgers, mobility, block_cells, pairs, pair_count):
    count_segs = positions.shape[1]
    width = BLOCK_SEGS
    n_slab = lax.axis_size("slab")
    n_dom = lax.axis_size("dom")
    ncells = 16 * n_slab
    blk_dev = block_cells.shape[0]
    far_scale = math.sqrt(ncells / (count_segs * n_slab * n_dom))
    slots = pairs.shape[0]
    my_slab = lax.axis_index("slab")
    my_dom = lax.axis_index("dom")
    used = pair_count[0]

    def locate(rotation_slots):
        return pairs[jnp.minimum(rotation_slots, slots - 1)]

    def to_window(blocks):
        owner = blocks // blk_dev
        within = blocks % blk_dev
        row_off = owner // n_dom - my_slab + 1
        col_off = owner % n_dom - my_dom + 1
        return jnp.clip((row_off * 3 + col_off) * blk_dev + within, 0, 9 * blk_dev - 1)

    def near(window):
        pos_win = window[0:3].reshape(3, -1, width)
        bur_win = window[3:6].reshape(3, -1, width)

        def turn(index, acc):
            rotation_slots = index * pair_batch + jnp.arange(pair_batch, dtype=jnp.int32)
            weight = (rotation_slots < used).astype(jnp.float32)
            chosen = locate(rotation_slots)
            first_blk = to_window(chosen[:, 0])
            second_blk = to_window(chosen[:, 1])
            force_a, force_b = pair_forces(
                pos_win[:, first_blk],
                bur_win[:, first_blk],
                pos_win[:, second_blk],
                bur_win[:, second_blk],
                weight,
            )
            return acc.at[:, first_blk].add(force_a).at[:, second_blk].add(force_b)

        groups = (used + pair_batch - 1) // pair_batch
        start = jnp.zeros(pos_win.shape, jnp.float32)
        return lax.fori_loop(0, groups, turn, start).reshape(3, -1)

    def gather_moments(posit):
        local = block_moments(posit, burgers, block_cells, 16, width, 16 * my_slab)
        summed = lax.psum(local, "dom")
        return lax.all_gather(summed, "slab", axis=1, tiled=True)

    def speed(posit, window):
        moments = gather_moments(posit)
        far = far_field(posit, burgers, moments)
        near_own = give_around(near(window), count_segs)
        return mobility[None, :] * (far_scale * far + near_own)

    stacked = jnp.concatenate([positions, burgers], axis=0)
    leading_window = around_all(stacked)
    first_v = speed(positions, leading_window)
    stepped = positions + time_increment * first_v
    restacked = jnp.concatenate([stepped, burgers], axis=0)
    window_second = around_all(restacked)
    second_v = speed(stepped, window_second)
    total = first_v + second_v
    return (positions + 0.5 * time_increment * total, 0.5 * total)


def solution(mesh):
    placed = (
        P(None, ("slab", "dom")),
        P(None, ("slab", "dom")),
        P(("slab", "dom")),
        P(("slab", "dom")),
        P(("slab", "dom"), None),
        P(("slab", "dom")),
    )
    return jax.shard_map(
        body,
        mesh=mesh,
        in_specs=placed,
        out_specs=(P(None, ("slab", "dom")), P(None, ("slab", "dom"))),
        check_vma=False,
    )
```

profile of v0, /device:TPU:0, one launch (start us, length us, event | category | flops | bytes accessed | tf_op | source)
XLA Modules:
  0.0 326.1 jit_solution(1120146685088651747)
XLA Ops:
  1.4 1.3 collective-permute-start.1
  2.6 3.0 collective-permute-start
  8.4 1.3 collective-permute-start.3
  9.7 5.5 %collective-permute-start.2 = (f32[6,3,1,512]{3,0,2,1:T(8,128)S(1)}, f32[6,3,1,512]{3,0,2,1:T(8,128)S(1)}, u32[]{:S(2)}, u32[]{:S(2)}) collective-permute-start(f32[6,3,1,512]{3,0,2,1:T(8,128)S(1)} %pad_maximum_fusion.4), channel_id=1, source_target_pairs={{0,1},{1,2},{2,3},{4,5},{5,6},{6,7},{8,9},{9,10},{10,11},{12,13},{... | collective-permute-start | bytes 110600 | tf_op jit(solution)/shard_map/ppermute | solution.py:22
  17.0 105.3 %while.48 = (s32[]{:T(128)}, f32[3,36,128]{2,0,1:T(4,128)S(1)}, s32[]{:T(128)}, s32[64,2]{1,0:T(8,128)S(1)}, s32[]{:T(128)}, /*index=5*/s32[]{:T(128)}, s32[]{:T...) while((s32[]{:T(128)}, f32[3,36,128]{2,0,1:T(4,128)S(1)}, ...), condition=%wide.region_14.15_spmd, body=%wide.region_8.14_spmd.sunk | while | flops 2233267 | bytes 2855389 | solution.py:157
  122.3 1.3 collective-permute-start.4
  123.6 3.0 collective-permute-start.5
  126.7 11.5 %psum.14 = f32[39,16]{0,1:T(8,128)S(1)} all-reduce(f32[39,16]{0,1:T(8,128)S(1)} %fusion.151), channel_id=1, replica_groups=mesh['slab'=8,'dom'=4] {'dom'}, use_global_device_ids=true, to_apply=%region_1.2 | all-reduce | flops 624 | bytes 4992 | tf_op jit(solution)/shard_map/psum | solution.py:161
  138.2 14.7 %all_gather.6 = f32[39,128]{0,1:T(8,128)S(1)} all-gather(f32[39,16]{0,1:T(8,128)S(1)} %psum.14), channel_id=1, replica_groups=mesh['slab'=8,'dom'=4] {'slab'}, dimensions={1}, use_global_device_ids=true | all-gather | bytes 22464 | tf_op jit(solution)/shard_map/all_gather | solution.py:162
  153.0 1.3 collective-permute-start.6
  154.3 4.5 %collective-permute-start.7 = (f32[3,512]{1,0:T(4,128)S(1)}, f32[3,512]{1,0:T(4,128)S(1)}, u32[]{:S(2)}, u32[]{:S(2)}) collective-permute-start(f32[3,512]{1,0:T(4,128)S(1)} %get-tuple-element.575), channel_id=1, source_target_pairs={{0,1},{1,2},{2,3},{4,5},{5,6},{6,7},{8,9},{9,10},{10,11},{12,13},{... | collective-permute-start | bytes 18440 | tf_op jit(solution)/shard_map/ppermute | solution.py:31
  158.9 5.3 %while.50 = (s32[]{:T(128)}, f32[3,512]{1,0:T(4,128)S(1)}, f32[3,512]{1,0:T(4,128)S(1)}, f32[2,3,64]{2,1,0:T(4,128)S(1)}, f32[2,39,64]{2,1,0:T(8,128)S(1)}, /*in...) while((s32[]{:T(128)}, f32[3,512]{1,0:T(4,128)S(1)}, f32[3,512]{1,0:T(4,128)S(1)}, ...), condition=%wide.region_7.8_spmd.clone, body=%wide.region_2.7_spmd.clone.sunk | while | flops 18023940 | bytes 6538151 | solution.py:82
  164.3 1.3 collective-permute-start.9
  165.6 3.0 collective-permute-start.8
  170.7 4.5 %collective-permute-start.10 = (f32[6,3,1,512]{3,0,2,1:T(8,128)S(1)}, f32[6,3,1,512]{3,0,2,1:T(8,128)S(1)}, u32[]{:S(2)}, u32[]{:S(2)}) collective-permute-start(f32[6,3,1,512]{3,0,2,1:T(8,128)S(1)} %pad_maximum_fusion.5), channel_id=1, source_target_pairs={{0,1},{1,2},{2,3},{4,5},{5,6},{6,7},{8,9},{9,10},{10,11},{12,13},{... | collective-permute-start | bytes 110600 | tf_op jit(solution)/shard_map/ppermute | solution.py:22
  175.6 1.7 collective-permute-done.10
  177.4 105.3 %while.49 = (s32[]{:T(128)}, f32[3,36,128]{2,0,1:T(4,128)S(1)}, s32[]{:T(128)}, s32[64,2]{1,0:T(8,128)S(1)}, s32[]{:T(128)}, /*index=5*/s32[]{:T(128)}, s32[]{:T...) while((s32[]{:T(128)}, f32[3,36,128]{2,0,1:T(4,128)S(1)}, ...), condition=%wide.region_29.30_spmd, body=%wide.region_23.29_spmd.sunk | while | flops 2233267 | bytes 2855389 | solution.py:157
  282.7 1.3 collective-permute-start.12
  284.0 3.0 collective-permute-start.13
  287.3 10.0 %psum.15 = f32[39,16]{0,1:T(8,128)S(1)} all-reduce(f32[39,16]{0,1:T(8,128)S(1)} %fusion.150), channel_id=1, replica_groups=mesh['slab'=8,'dom'=4] {'dom'}, use_global_device_ids=true, to_apply=%region_16.17 | all-reduce | flops 624 | bytes 4992 | tf_op jit(solution)/shard_map/psum | solution.py:161
  297.3 16.3 %all_gather.7 = f32[39,128]{0,1:T(8,128)S(1)} all-gather(f32[39,16]{0,1:T(8,128)S(1)} %psum.15), channel_id=1, replica_groups=mesh['slab'=8,'dom'=4] {'slab'}, dimensions={1}, use_global_device_ids=true | all-gather | bytes 22464 | tf_op jit(solution)/shard_map/all_gather | solution.py:162
  313.7 1.3 collective-permute-start.14
  315.0 4.5 %collective-permute-start.15 = (f32[3,512]{1,0:T(4,128)S(1)}, f32[3,512]{1,0:T(4,128)S(1)}, u32[]{:S(2)}, u32[]{:S(2)}) collective-permute-start(f32[3,512]{1,0:T(4,128)S(1)} %get-tuple-element.573), channel_id=1, source_target_pairs={{0,1},{1,2},{2,3},{4,5},{5,6},{6,7},{8,9},{9,10},{10,11},{12,13},{... | collective-permute-start | bytes 18440 | tf_op jit(solution)/shard_map/ppermute | solution.py:31
  319.5 5.3 %while.51 = (s32[]{:T(128)}, f32[3,512]{1,0:T(4,128)S(1)}, f32[3,512]{1,0:T(4,128)S(1)}, f32[2,3,64]{2,1,0:T(4,128)S(1)}, f32[2,39,64]{2,1,0:T(8,128)S(1)}, /*in...) while((s32[]{:T(128)}, f32[3,512]{1,0:T(4,128)S(1)}, f32[3,512]{1,0:T(4,128)S(1)}, ...), condition=%wide.region_22.23_spmd.clone, body=%wide.region_17.22_spmd.clone.sunk | while | flops 18023940 | bytes 6538151 | solution.py:82
  (854 shorter events, 226.7 us)
Async XLA Ops:
  1.4 7.0 %collective-permute-start.1 = (f32[6,1,1,512]{3,0,2,1:T(8,128)S(1)}, f32[6,1,1,512]{3,0,2,1:T(8,128)S(1)}, u32[]{:S(2)}, u32[]{:S(2)}) collective-permute-start(f32[6,1,1,512]{3,0,2,1:T(8,128)S(1)} %fusion.138), channel_id=1, source_target_pairs={{4,0},{8,4},{12,8},{16,12},{20,16},{24,20},{28,24},{5,1},{9,5},{13... | collective-permute-start | bytes 36872 | tf_op jit(solution)/shard_map/ppermute | solution.py:23
  2.6 5.7 %collective-permute-start = (f32[6,1,1,512]{3,0,2,1:T(8,128)S(1)}, f32[6,1,1,512]{3,0,2,1:T(8,128)S(1)}, u32[]{:S(2)}, u32[]{:S(2)}) collective-permute-start(f32[6,1,1,512]{3,0,2,1:T(8,128)S(1)} %fusion.138), channel_id=1, source_target_pairs={{0,4},{4,8},{8,12},{12,16},{16,20},{20,24},{24,28},{1,5},{5,9},{9,... | collective-permute-start | bytes 36872 | tf_op jit(solution)/shard_map/ppermute | solution.py:22
  8.4 8.3 %collective-permute-start.3 = (f32[6,3,1,512]{3,0,2,1:T(8,128)S(1)}, f32[6,3,1,512]{3,0,2,1:T(8,128)S(1)}, u32[]{:S(2)}, u32[]{:S(2)}) collective-permute-start(f32[6,3,1,512]{3,0,2,1:T(8,128)S(1)} %pad_maximum_fusion.4), channel_id=1, source_target_pairs={{1,0},{2,1},{3,2},{5,4},{6,5},{7,6},{9,8},{10,9},{11,10},{13,12},{... | collective-permute-start | bytes 110600 | tf_op jit(solution)/shard_map/ppermute | solution.py:23
  9.7 7.2 %collective-permute-start.2 = (f32[6,3,1,512]{3,0,2,1:T(8,128)S(1)}, f32[6,3,1,512]{3,0,2,1:T(8,128)S(1)}, u32[]{:S(2)}, u32[]{:S(2)}) collective-permute-start(f32[6,3,1,512]{3,0,2,1:T(8,128)S(1)} %pad_maximum_fusion.4), channel_id=1, source_target_pairs={{0,1},{1,2},{2,3},{4,5},{5,6},{6,7},{8,9},{9,10},{10,11},{12,13},{... | collective-permute-start | bytes 110600 | tf_op jit(solution)/shard_map/ppermute | solution.py:22
  17.0 141.9 %copy-start = (f32[3,512]{1,0:T(4,128)S(1)}, f32[3,512]{1,0:T(4,128)}, u32[]{:S(2)}) copy-start(f32[3,512]{1,0:T(4,128)} %param.15) | copy-start | bytes 18436
  17.0 141.9 %copy-start.1 = (f32[3,512]{1,0:T(4,128)S(1)}, f32[3,512]{1,0:T(4,128)}, u32[]{:S(2)}) copy-start(f32[3,512]{1,0:T(4,128)} %param.14) | copy-start | bytes 18436
  122.3 30.6 %collective-permute-start.4 = (f32[3,3,512]{2,0,1:T(4,128)S(1)}, f32[3,3,512]{2,0,1:T(4,128)S(1)}, u32[]{:S(2)}, u32[]{:S(2)}) collective-permute-start(f32[3,3,512]{2,0,1:T(4,128)S(1)} %get-tuple-element.570), channel_id=1, source_target_pairs={{4,0},{8,4},{12,8},{16,12},{20,16},{24,20},{28,24},{5,1},{9,5},{13... | collective-permute-start | bytes 55304 | tf_op jit(solution)/shard_map/ppermute | solution.py:31
  123.6 29.3 %collective-permute-start.5 = (f32[3,3,512]{2,0,1:T(4,128)S(1)}, f32[3,3,512]{2,0,1:T(4,128)S(1)}, u32[]{:S(2)}, u32[]{:S(2)}) collective-permute-start(f32[3,3,512]{2,0,1:T(4,128)S(1)} %get-tuple-element.571), channel_id=1, source_target_pairs={{0,4},{4,8},{8,12},{12,16},{16,20},{20,24},{24,28},{1,5},{5,9},{9,... | collective-permute-start | bytes 55304 | tf_op jit(solution)/shard_map/ppermute | solution.py:31
  153.0 11.2 %collective-permute-start.6 = (f32[3,512]{1,0:T(4,128)S(1)}, f32[3,512]{1,0:T(4,128)S(1)}, u32[]{:S(2)}, u32[]{:S(2)}) collective-permute-start(f32[3,512]{1,0:T(4,128)S(1)} %get-tuple-element.574), channel_id=1, source_target_pairs={{1,0},{2,1},{3,2},{5,4},{6,5},{7,6},{9,8},{10,9},{11,10},{13,12},{... | collective-permute-start | bytes 18440 | tf_op jit(solution)/shard_map/ppermute | solution.py:31
  154.3 9.9 %collective-permute-start.7 = (f32[3,512]{1,0:T(4,128)S(1)}, f32[3,512]{1,0:T(4,128)S(1)}, u32[]{:S(2)}, u32[]{:S(2)}) collective-permute-start(f32[3,512]{1,0:T(4,128)S(1)} %get-tuple-element.575), channel_id=1, source_target_pairs={{0,1},{1,2},{2,3},{4,5},{5,6},{6,7},{8,9},{9,10},{10,11},{12,13},{... | collective-permute-start | bytes 18440 | tf_op jit(solution)/shard_map/ppermute | solution.py:31
  158.8 5.4 %copy-start.2 = (f32[512]{0:T(512)S(1)}, f32[512]{0:T(512)}, u32[]{:S(2)}) copy-start(f32[512]{0:T(512)} %param.16) | copy-start | bytes 6148
  164.3 4.4 %collective-permute-start.9 = (f32[6,1,1,512]{3,0,2,1:T(8,128)S(1)}, f32[6,1,1,512]{3,0,2,1:T(8,128)S(1)}, u32[]{:S(2)}, u32[]{:S(2)}) collective-permute-start(f32[6,1,1,512]{3,0,2,1:T(8,128)S(1)} %fusion.139), channel_id=1, source_target_pairs={{4,0},{8,4},{12,8},{16,12},{20,16},{24,20},{28,24},{5,1},{9,5},{13... | collective-permute-start | bytes 36872 | tf_op jit(solution)/shard_map/ppermute | solution.py:23
  165.6 3.9 %collective-permute-start.8 = (f32[6,1,1,512]{3,0,2,1:T(8,128)S(1)}, f32[6,1,1,512]{3,0,2,1:T(8,128)S(1)}, u32[]{:S(2)}, u32[]{:S(2)}) collective-permute-start(f32[6,1,1,512]{3,0,2,1:T(8,128)S(1)} %fusion.139), channel_id=1, source_target_pairs={{0,4},{4,8},{8,12},{12,16},{16,20},{20,24},{24,28},{1,5},{5,9},{9,... | collective-permute-start | bytes 36872 | tf_op jit(solution)/shard_map/ppermute | solution.py:22
  169.4 6.1 %collective-permute-start.11 = (f32[6,3,1,512]{3,0,2,1:T(8,128)S(1)}, f32[6,3,1,512]{3,0,2,1:T(8,128)S(1)}, u32[]{:S(2)}, u32[]{:S(2)}) collective-permute-start(f32[6,3,1,512]{3,0,2,1:T(8,128)S(1)} %pad_maximum_fusion.5), channel_id=1, source_target_pairs={{1,0},{2,1},{3,2},{5,4},{6,5},{7,6},{9,8},{10,9},{11,10},{13,12},{... | collective-permute-start | bytes 110600 | tf_op jit(solution)/shard_map/ppermute | solution.py:23
  170.7 6.6 %collective-permute-start.10 = (f32[6,3,1,512]{3,0,2,1:T(8,128)S(1)}, f32[6,3,1,512]{3,0,2,1:T(8,128)S(1)}, u32[]{:S(2)}, u32[]{:S(2)}) collective-permute-start(f32[6,3,1,512]{3,0,2,1:T(8,128)S(1)} %pad_maximum_fusion.5), channel_id=1, source_target_pairs={{0,1},{1,2},{2,3},{4,5},{5,6},{6,7},{8,9},{9,10},{10,11},{12,13},{... | collective-permute-start | bytes 110600 | tf_op jit(solution)/shard_map/ppermute | solution.py:22
  282.7 30.9 %collective-permute-start.12 = (f32[3,3,512]{2,0,1:T(4,128)S(1)}, f32[3,3,512]{2,0,1:T(4,128)S(1)}, u32[]{:S(2)}, u32[]{:S(2)}) collective-permute-start(f32[3,3,512]{2,0,1:T(4,128)S(1)} %get-tuple-element.568), channel_id=1, source_target_pairs={{4,0},{8,4},{12,8},{16,12},{20,16},{24,20},{28,24},{5,1},{9,5},{13... | collective-permute-start | bytes 55304 | tf_op jit(solution)/shard_map/ppermute | solution.py:31
  284.0 29.6 %collective-permute-start.13 = (f32[3,3,512]{2,0,1:T(4,128)S(1)}, f32[3,3,512]{2,0,1:T(4,128)S(1)}, u32[]{:S(2)}, u32[]{:S(2)}) collective-permute-start(f32[3,3,512]{2,0,1:T(4,128)S(1)} %get-tuple-element.569), channel_id=1, source_target_pairs={{0,4},{4,8},{8,12},{12,16},{16,20},{20,24},{24,28},{1,5},{5,9},{9,... | collective-permute-start | bytes 55304 | tf_op jit(solution)/shard_map/ppermute | solution.py:31
  313.7 11.2 %collective-permute-start.14 = (f32[3,512]{1,0:T(4,128)S(1)}, f32[3,512]{1,0:T(4,128)S(1)}, u32[]{:S(2)}, u32[]{:S(2)}) collective-permute-start(f32[3,512]{1,0:T(4,128)S(1)} %get-tuple-element.572), channel_id=1, source_target_pairs={{1,0},{2,1},{3,2},{5,4},{6,5},{7,6},{9,8},{10,9},{11,10},{13,12},{... | collective-permute-start | bytes 18440 | tf_op jit(solution)/shard_map/ppermute | solution.py:31
  315.0 9.9 %collective-permute-start.15 = (f32[3,512]{1,0:T(4,128)S(1)}, f32[3,512]{1,0:T(4,128)S(1)}, u32[]{:S(2)}, u32[]{:S(2)}) collective-permute-start(f32[3,512]{1,0:T(4,128)S(1)} %get-tuple-element.573), channel_id=1, source_target_pairs={{0,1},{1,2},{2,3},{4,5},{5,6},{6,7},{8,9},{9,10},{10,11},{12,13},{... | collective-permute-start | bytes 18440 | tf_op jit(solution)/shard_map/ppermute | solution.py:31
where the time goes:
time: 327 us; the launch traced here: 326 us
  other arithmetic  121 us (37%)
  local copies, waits for them, and re-layouts  94.8 us (29%)
  blocking collectives  52.4 us (16%)
  starting transfers between devices  41.6 us (13%)
  matrix products  8.84 us (3%)
    scatter-add x64, other arithmetic, turn(): return acc.at[:, first_blk].add(force_a).at[:, second_blk].add(force_b)  41.4 us
    all_gather x2, blocking collectives, gather_moments(): return lax.all_gather(summed, 'slab', axis=1, tiled=True)  30.9 us
    psum x2, blocking collectives, gather_moments(): summed = lax.psum(local, 'dom')  21.4 us
    convert_element_type x32, other arithmetic, turn(): weight = (rotation_slots < used).astype(jnp.float32)  20.8 us
    ppermute x8, starting transfers between devices, shifted(): return lax.ppermute(block, axis, route)  20.3 us
    gather x64, local copies, waits for them, and re-layouts, turn(): pos_win[:, second_blk]  18.5 us
    gather x64, local copies, waits for them, and re-layouts, turn(): bur_win[:, first_blk]  18.4 us
    gather x64, local copies, waits for them, and re-layouts, turn(): bur_win[:, second_blk]  18.4 us
  transfers between devices with their start and end apart: 16, of which 4 were waited for; matrix products, arithmetic and copies ran while one was open for 4% of the time, Pallas kernels for 0%

commit v1 on v0

--- a/solution.py
+++ b/solution.py
@@ -158,7 +158,9 @@
 
     def gather_moments(posit):
         local = block_moments(posit, burgers, block_cells, 16, width, 16 * my_slab)
-        summed = lax.psum(local, "dom")
+        summed = local
+        for hop in (1, 2):
+            summed = summed + lax.ppermute(summed, "dom", [(dev, dev ^ hop) for dev in range(4)])
         return lax.all_gather(summed, "slab", axis=1, tiled=True)
 
     def speed(posit, window):

time: 327 us -> 317 us (0.969)
  blocking collectives: 52.4 us -> 31.3 us
  waiting for transfers between devices: 2.92 us -> 8.27 us
  starting transfers between devices: 41.6 us -> 46.8 us
    psum x2 -> x0, blocking collectives: 21.4 us -> none  [gather_moments(): summed = lax.psum(local, 'dom')]
    ppermute x0 -> x4, starting transfers between devices: none -> 6.17 us  [gather_moments(): lax.ppermute(summed, 'dom', [(dev, dev ^ hop) for dev in range(4)])]
    ppermute x0 -> x4, waiting for transfers between devices: none -> 5.73 us  [gather_moments(): lax.ppermute(summed, 'dom', [(dev, dev ^ hop) for dev in range(4)])]
  transfers between devices with their start and end apart: 16 -> 20, of which waited for: 4 -> 5; matrix products, arithmetic and copies ran while one was open for 4% -> 37% of each run, Pallas kernels for 0% -> 0%
where the time goes in v1:
time: 317 us; the launch traced here: 316 us
  other arithmetic  121 us (38%)
  local copies, waits for them, and re-layouts  94.8 us (30%)
  starting transfers between devices  46.8 us (15%)
  blocking collectives  31.3 us (10%)
  matrix products  8.84 us (3%)
  waiting for transfers between devices  8.27 us (3%)
    scatter-add x64, other arithmetic, turn(): return acc.at[:, first_blk].add(force_a).at[:, second_blk].add(force_b)  41.4 us
    all_gather x2, blocking collectives, gather_moments(): return lax.all_gather(summed, 'slab', axis=1, tiled=True)  31.3 us
    convert_element_type x32, other arithmetic, turn(): weight = (rotation_slots < used).astype(jnp.float32)  20.8 us
    ppermute x8, starting transfers between devices, shifted(): return lax.ppermute(block, axis, route)  20.3 us
    gather x64, local copies, waits for them, and re-layouts, turn(): pos_win[:, second_blk]  18.5 us
    gather x64, local copies, waits for them, and re-layouts, turn(): pos_win[:, first_blk]  18.4 us
    gather x64, local copies, waits for them, and re-layouts, turn(): bur_win[:, first_blk]  18.4 us
    gather x64, local copies, waits for them, and re-layouts, turn(): bur_win[:, second_blk]  18.4 us
  transfers between devices with their start and end apart: 20, of which 5 were waited for; matrix products, arithmetic and copies ran while one was open for 37% of the time, Pallas kernels for 0%

profile of v1, /device:TPU:0, one launch (start us, length us, event | category | flops | bytes accessed | tf_op | source)
XLA Modules:
  0.0 315.6 jit_solution(2632499617565949049)
XLA Ops:
  2.6 3.0 collective-permute-start.2
  8.3 3.0 collective-permute-start
  11.3 1.3 collective-permute-start.5
  12.6 4.5 %collective-permute-start.4 = (f32[6,3,1,512]{3,0,2,1:T(8,128)S(1)}, f32[6,3,1,512]{3,0,2,1:T(8,128)S(1)}, u32[]{:S(2)}, u32[]{:S(2)}) collective-permute-start(f32[6,3,1,512]{3,0,2,1:T(8,128)S(1)} %pad_maximum_fusion.4), channel_id=1, source_target_pairs={{0,1},{1,2},{2,3},{4,5},{5,6},{6,7},{8,9},{9,10},{10,11},{12,13},{... | collective-permute-start | bytes 110600 | tf_op jit(solution)/shard_map/ppermute | solution.py:22
  18.6 1.6 collective-permute-start.1
  20.3 105.3 %while.48 = (s32[]{:T(128)}, f32[3,36,128]{2,0,1:T(4,128)S(1)}, s32[]{:T(128)}, s32[64,2]{1,0:T(8,128)S(1)}, s32[]{:T(128)}, /*index=5*/s32[]{:T(128)}, s32[]{:T...) while((s32[]{:T(128)}, f32[3,36,128]{2,0,1:T(4,128)S(1)}, ...), condition=%wide.region_13.14_spmd, body=%wide.region_7.13_spmd.sunk | while | flops 2233267 | bytes 2855389 | solution.py:157
  125.7 1.3 collective-permute-start.6
  127.0 3.0 collective-permute-start.7
  130.1 14.0 %all_gather.6 = f32[39,128]{0,1:T(8,128)S(1)} all-gather(f32[39,16]{0,1:T(8,128)S(1)} %add.742), channel_id=1, replica_groups=mesh['slab'=8,'dom'=4] {'slab'}, dimensions={1}, use_global_device_ids=true | all-gather | bytes 22464 | tf_op jit(solution)/shard_map/all_gather | solution.py:164
  144.2 1.3 collective-permute-start.8
  145.5 4.5 %collective-permute-start.9 = (f32[3,512]{1,0:T(4,128)S(1)}, f32[3,512]{1,0:T(4,128)S(1)}, u32[]{:S(2)}, u32[]{:S(2)}) collective-permute-start(f32[3,512]{1,0:T(4,128)S(1)} %get-tuple-element.575), channel_id=1, source_target_pairs={{0,1},{1,2},{2,3},{4,5},{5,6},{6,7},{8,9},{9,10},{10,11},{12,13},{... | collective-permute-start | bytes 18440 | tf_op jit(solution)/shard_map/ppermute | solution.py:31
  150.1 5.3 %while.50 = (s32[]{:T(128)}, f32[3,512]{1,0:T(4,128)S(1)}, f32[3,512]{1,0:T(4,128)S(1)}, f32[2,3,64]{2,1,0:T(4,128)S(1)}, f32[2,39,64]{2,1,0:T(8,128)S(1)}, /*in...) while((s32[]{:T(128)}, f32[3,512]{1,0:T(4,128)S(1)}, f32[3,512]{1,0:T(4,128)S(1)}, ...), condition=%wide.region_6.7_spmd.clone, body=%wide.region_1.6_spmd.clone.sunk | while | flops 18023940 | bytes 6538151 | solution.py:82
  155.5 1.3 collective-permute-start.13
  156.8 3.0 collective-permute-start.12
  161.9 4.5 %collective-permute-start.14 = (f32[6,3,1,512]{3,0,2,1:T(8,128)S(1)}, f32[6,3,1,512]{3,0,2,1:T(8,128)S(1)}, u32[]{:S(2)}, u32[]{:S(2)}) collective-permute-start(f32[6,3,1,512]{3,0,2,1:T(8,128)S(1)} %pad_maximum_fusion.5), channel_id=1, source_target_pairs={{0,1},{1,2},{2,3},{4,5},{5,6},{6,7},{8,9},{9,10},{10,11},{12,13},{... | collective-permute-start | bytes 110600 | tf_op jit(solution)/shard_map/ppermute | solution.py:22
  167.1 1.3 collective-permute-done.14
  168.5 105.3 %while.49 = (s32[]{:T(128)}, f32[3,36,128]{2,0,1:T(4,128)S(1)}, s32[]{:T(128)}, s32[64,2]{1,0:T(8,128)S(1)}, s32[]{:T(128)}, /*index=5*/s32[]{:T(128)}, s32[]{:T...) while((s32[]{:T(128)}, f32[3,36,128]{2,0,1:T(4,128)S(1)}, ...), condition=%wide.region_27.28_spmd, body=%wide.region_21.27_spmd.sunk | while | flops 2233267 | bytes 2855389 | solution.py:157
  275.1 3.0 collective-permute-start.17
  278.4 3.7 %collective-permute-done.10 = f32[39,16]{0,1:T(8,128)S(1)} collective-permute-done((f32[39,16]{0,1:T(8,128)S(1)}, f32[39,16]{0,1:T(8,128)S(1)}, u32[]{:S(2)}, u32[]{:S(2)}) %collective-permute-start.10) | collective-permute-done | bytes 2528 | tf_op jit(solution)/shard_map/ppermute | solution.py:163
  282.1 1.6 collective-permute-start.11
  283.7 2.1 collective-permute-done.11
  285.7 17.3 %all_gather.7 = f32[39,128]{0,1:T(8,128)S(1)} all-gather(f32[39,16]{0,1:T(8,128)S(1)} %add.750), channel_id=1, replica_groups=mesh['slab'=8,'dom'=4] {'slab'}, dimensions={1}, use_global_device_ids=true | all-gather | bytes 22464 | tf_op jit(solution)/shard_map/all_gather | solution.py:164
  304.5 4.5 %collective-permute-start.19 = (f32[3,512]{1,0:T(4,128)S(1)}, f32[3,512]{1,0:T(4,128)S(1)}, u32[]{:S(2)}, u32[]{:S(2)}) collective-permute-start(f32[3,512]{1,0:T(4,128)S(1)} %get-tuple-element.573), channel_id=1, source_target_pairs={{0,1},{1,2},{2,3},{4,5},{5,6},{6,7},{8,9},{9,10},{10,11},{12,13},{... | collective-permute-start | bytes 18440 | tf_op jit(solution)/shard_map/ppermute | solution.py:31
  309.1 5.3 %while.51 = (s32[]{:T(128)}, f32[3,512]{1,0:T(4,128)S(1)}, f32[3,512]{1,0:T(4,128)S(1)}, f32[2,3,64]{2,1,0:T(4,128)S(1)}, f32[2,39,64]{2,1,0:T(8,128)S(1)}, /*in...) while((s32[]{:T(128)}, f32[3,512]{1,0:T(4,128)S(1)}, f32[3,512]{1,0:T(4,128)S(1)}, ...), condition=%wide.region_20.21_spmd.clone, body=%wide.region_15.20_spmd.clone.sunk | while | flops 18023940 | bytes 6538151 | solution.py:82
  (864 shorter events, 230.6 us)
Async XLA Ops:
  1.4 9.9 %collective-permute-start.3 = (f32[6,1,1,512]{3,0,2,1:T(8,128)S(1)}, f32[6,1,1,512]{3,0,2,1:T(8,128)S(1)}, u32[]{:S(2)}, u32[]{:S(2)}) collective-permute-start(f32[6,1,1,512]{3,0,2,1:T(8,128)S(1)} %fusion.138), channel_id=1, source_target_pairs={{4,0},{8,4},{12,8},{16,12},{20,16},{24,20},{28,24},{5,1},{9,5},{13... | collective-permute-start | bytes 36872 | tf_op jit(solution)/shard_map/ppermute | solution.py:23
  2.6 8.7 %collective-permute-start.2 = (f32[6,1,1,512]{3,0,2,1:T(8,128)S(1)}, f32[6,1,1,512]{3,0,2,1:T(8,128)S(1)}, u32[]{:S(2)}, u32[]{:S(2)}) collective-permute-start(f32[6,1,1,512]{3,0,2,1:T(8,128)S(1)} %fusion.138), channel_id=1, source_target_pairs={{0,4},{4,8},{8,12},{12,16},{16,20},{20,24},{24,28},{1,5},{5,9},{9,... | collective-permute-start | bytes 36872 | tf_op jit(solution)/shard_map/ppermute | solution.py:22
  8.3 10.3 %collective-permute-start = (f32[39,16]{0,1:T(8,128)S(1)}, f32[39,16]{0,1:T(8,128)S(1)}, u32[]{:S(2)}, u32[]{:S(2)}) collective-permute-start(f32[39,16]{0,1:T(8,128)S(1)} %fusion.151), channel_id=1, source_target_pairs={{0,1},{1,0},{2,3},{3,2},{4,5},{5,4},{6,7},{7,6},{8,9},{9,8},{10,11... | collective-permute-start | bytes 7496 | tf_op jit(solution)/shard_map/ppermute | solution.py:163
  11.3 8.9 %collective-permute-start.5 = (f32[6,3,1,512]{3,0,2,1:T(8,128)S(1)}, f32[6,3,1,512]{3,0,2,1:T(8,128)S(1)}, u32[]{:S(2)}, u32[]{:S(2)}) collective-permute-start(f32[6,3,1,512]{3,0,2,1:T(8,128)S(1)} %pad_maximum_fusion.4), channel_id=1, source_target_pairs={{1,0},{2,1},{3,2},{5,4},{6,5},{7,6},{9,8},{10,9},{11,10},{13,12},{... | collective-permute-start | bytes 110600 | tf_op jit(solution)/shard_map/ppermute | solution.py:23
  12.6 7.6 %collective-permute-start.4 = (f32[6,3,1,512]{3,0,2,1:T(8,128)S(1)}, f32[6,3,1,512]{3,0,2,1:T(8,128)S(1)}, u32[]{:S(2)}, u32[]{:S(2)}) collective-permute-start(f32[6,3,1,512]{3,0,2,1:T(8,128)S(1)} %pad_maximum_fusion.4), channel_id=1, source_target_pairs={{0,1},{1,2},{2,3},{4,5},{5,6},{6,7},{8,9},{9,10},{10,11},{12,13},{... | collective-permute-start | bytes 110600 | tf_op jit(solution)/shard_map/ppermute | solution.py:22
  18.6 111.4 %collective-permute-start.1 = (f32[39,16]{0,1:T(8,128)S(1)}, f32[39,16]{0,1:T(8,128)S(1)}, u32[]{:S(2)}, u32[]{:S(2)}) collective-permute-start(f32[39,16]{0,1:T(8,128)S(1)} %add.741), channel_id=1, source_target_pairs={{0,2},{1,3},{2,0},{3,1},{4,6},{5,7},{6,4},{7,5},{8,10},{9,11},{10,... | collective-permute-start | bytes 7496 | tf_op jit(solution)/shard_map/ppermute | solution.py:163
  20.3 129.7 %copy-start = (f32[3,512]{1,0:T(4,128)S(1)}, f32[3,512]{1,0:T(4,128)}, u32[]{:S(2)}) copy-start(f32[3,512]{1,0:T(4,128)} %param.15) | copy-start | bytes 18436
  20.3 129.7 %copy-start.1 = (f32[3,512]{1,0:T(4,128)S(1)}, f32[3,512]{1,0:T(4,128)}, u32[]{:S(2)}) copy-start(f32[3,512]{1,0:T(4,128)} %param.14) | copy-start | bytes 18436
  125.7 18.5 %collective-permute-start.6 = (f32[3,3,512]{2,0,1:T(4,128)S(1)}, f32[3,3,512]{2,0,1:T(4,128)S(1)}, u32[]{:S(2)}, u32[]{:S(2)}) collective-permute-start(f32[3,3,512]{2,0,1:T(4,128)S(1)} %get-tuple-element.570), channel_id=1, source_target_pairs={{4,0},{8,4},{12,8},{16,12},{20,16},{24,20},{28,24},{5,1},{9,5},{13... | collective-permute-start | bytes 55304 | tf_op jit(solution)/shard_map/ppermute | solution.py:31
  127.0 17.2 %collective-permute-start.7 = (f32[3,3,512]{2,0,1:T(4,128)S(1)}, f32[3,3,512]{2,0,1:T(4,128)S(1)}, u32[]{:S(2)}, u32[]{:S(2)}) collective-permute-start(f32[3,3,512]{2,0,1:T(4,128)S(1)} %get-tuple-element.571), channel_id=1, source_target_pairs={{0,4},{4,8},{8,12},{12,16},{16,20},{20,24},{24,28},{1,5},{5,9},{9,... | collective-permute-start | bytes 55304 | tf_op jit(solution)/shard_map/ppermute | solution.py:31
  144.2 11.2 %collective-permute-start.8 = (f32[3,512]{1,0:T(4,128)S(1)}, f32[3,512]{1,0:T(4,128)S(1)}, u32[]{:S(2)}, u32[]{:S(2)}) collective-permute-start(f32[3,512]{1,0:T(4,128)S(1)} %get-tuple-element.574), channel_id=1, source_target_pairs={{1,0},{2,1},{3,2},{5,4},{6,5},{7,6},{9,8},{10,9},{11,10},{13,12},{... | collective-permute-start | bytes 18440 | tf_op jit(solution)/shard_map/ppermute | solution.py:31
  145.5 9.9 %collective-permute-start.9 = (f32[3,512]{1,0:T(4,128)S(1)}, f32[3,512]{1,0:T(4,128)S(1)}, u32[]{:S(2)}, u32[]{:S(2)}) collective-permute-start(f32[3,512]{1,0:T(4,128)S(1)} %get-tuple-element.575), channel_id=1, source_target_pairs={{0,1},{1,2},{2,3},{4,5},{5,6},{6,7},{8,9},{9,10},{10,11},{12,13},{... | collective-permute-start | bytes 18440 | tf_op jit(solution)/shard_map/ppermute | solution.py:31
  150.1 5.3 %copy-start.2 = (f32[512]{0:T(512)S(1)}, f32[512]{0:T(512)}, u32[]{:S(2)}) copy-start(f32[512]{0:T(512)} %param.16) | copy-start | bytes 6148
  155.5 4.4 %collective-permute-start.13 = (f32[6,1,1,512]{3,0,2,1:T(8,128)S(1)}, f32[6,1,1,512]{3,0,2,1:T(8,128)S(1)}, u32[]{:S(2)}, u32[]{:S(2)}) collective-permute-start(f32[6,1,1,512]{3,0,2,1:T(8,128)S(1)} %fusion.139), channel_id=1, source_target_pairs={{4,0},{8,4},{12,8},{16,12},{20,16},{24,20},{28,24},{5,1},{9,5},{13... | collective-permute-start | bytes 36872 | tf_op jit(solution)/shard_map/ppermute | solution.py:23
  156.8 3.9 %collective-permute-start.12 = (f32[6,1,1,512]{3,0,2,1:T(8,128)S(1)}, f32[6,1,1,512]{3,0,2,1:T(8,128)S(1)}, u32[]{:S(2)}, u32[]{:S(2)}) collective-permute-start(f32[6,1,1,512]{3,0,2,1:T(8,128)S(1)} %fusion.139), channel_id=1, source_target_pairs={{0,4},{4,8},{8,12},{12,16},{16,20},{20,24},{24,28},{1,5},{5,9},{9,... | collective-permute-start | bytes 36872 | tf_op jit(solution)/shard_map/ppermute | solution.py:22
  160.6 6.4 %collective-permute-start.15 = (f32[6,3,1,512]{3,0,2,1:T(8,128)S(1)}, f32[6,3,1,512]{3,0,2,1:T(8,128)S(1)}, u32[]{:S(2)}, u32[]{:S(2)}) collective-permute-start(f32[6,3,1,512]{3,0,2,1:T(8,128)S(1)} %pad_maximum_fusion.5), channel_id=1, source_target_pairs={{1,0},{2,1},{3,2},{5,4},{6,5},{7,6},{9,8},{10,9},{11,10},{13,12},{... | collective-permute-start | bytes 110600 | tf_op jit(solution)/shard_map/ppermute | solution.py:23
  161.9 6.5 %collective-permute-start.14 = (f32[6,3,1,512]{3,0,2,1:T(8,128)S(1)}, f32[6,3,1,512]{3,0,2,1:T(8,128)S(1)}, u32[]{:S(2)}, u32[]{:S(2)}) collective-permute-start(f32[6,3,1,512]{3,0,2,1:T(8,128)S(1)} %pad_maximum_fusion.5), channel_id=1, source_target_pairs={{0,1},{1,2},{2,3},{4,5},{5,6},{6,7},{8,9},{9,10},{10,11},{12,13},{... | collective-permute-start | bytes 110600 | tf_op jit(solution)/shard_map/ppermute | solution.py:22
  273.8 29.4 %collective-permute-start.16 = (f32[3,3,512]{2,0,1:T(4,128)S(1)}, f32[3,3,512]{2,0,1:T(4,128)S(1)}, u32[]{:S(2)}, u32[]{:S(2)}) collective-permute-start(f32[3,3,512]{2,0,1:T(4,128)S(1)} %get-tuple-element.568), channel_id=1, source_target_pairs={{4,0},{8,4},{12,8},{16,12},{20,16},{24,20},{28,24},{5,1},{9,5},{13... | collective-permute-start | bytes 55304 | tf_op jit(solution)/shard_map/ppermute | solution.py:31
  275.1 28.1 %collective-permute-start.17 = (f32[3,3,512]{2,0,1:T(4,128)S(1)}, f32[3,3,512]{2,0,1:T(4,128)S(1)}, u32[]{:S(2)}, u32[]{:S(2)}) collective-permute-start(f32[3,3,512]{2,0,1:T(4,128)S(1)} %get-tuple-element.569), channel_id=1, source_target_pairs={{0,4},{4,8},{8,12},{12,16},{16,20},{20,24},{24,28},{1,5},{5,9},{9,... | collective-permute-start | bytes 55304 | tf_op jit(solution)/shard_map/ppermute | solution.py:31
  278.4 3.7 %collective-permute-start.10 = (f32[39,16]{0,1:T(8,128)S(1)}, f32[39,16]{0,1:T(8,128)S(1)}, u32[]{:S(2)}, u32[]{:S(2)}) collective-permute-start(f32[39,16]{0,1:T(8,128)S(1)} %fusion.150), channel_id=1, source_target_pairs={{0,1},{1,0},{2,3},{3,2},{4,5},{5,4},{6,7},{7,6},{8,9},{9,8},{10,11... | collective-permute-start | bytes 7496 | tf_op jit(solution)/shard_map/ppermute | solution.py:163
  282.1 3.7 %collective-permute-start.11 = (f32[39,16]{0,1:T(8,128)S(1)}, f32[39,16]{0,1:T(8,128)S(1)}, u32[]{:S(2)}, u32[]{:S(2)}) collective-permute-start(f32[39,16]{0,1:T(8,128)S(1)} %add.749), channel_id=1, source_target_pairs={{0,2},{1,3},{2,0},{3,1},{4,6},{5,7},{6,4},{7,5},{8,10},{9,11},{10,... | collective-permute-start | bytes 7496 | tf_op jit(solution)/shard_map/ppermute | solution.py:163
  303.2 11.2 %collective-permute-start.18 = (f32[3,512]{1,0:T(4,128)S(1)}, f32[3,512]{1,0:T(4,128)S(1)}, u32[]{:S(2)}, u32[]{:S(2)}) collective-permute-start(f32[3,512]{1,0:T(4,128)S(1)} %get-tuple-element.572), channel_id=1, source_target_pairs={{1,0},{2,1},{3,2},{5,4},{6,5},{7,6},{9,8},{10,9},{11,10},{13,12},{... | collective-permute-start | bytes 18440 | tf_op jit(solution)/shard_map/ppermute | solution.py:31
  304.5 9.9 %collective-permute-start.19 = (f32[3,512]{1,0:T(4,128)S(1)}, f32[3,512]{1,0:T(4,128)S(1)}, u32[]{:S(2)}, u32[]{:S(2)}) collective-permute-start(f32[3,512]{1,0:T(4,128)S(1)} %get-tuple-element.573), channel_id=1, source_target_pairs={{0,1},{1,2},{2,3},{4,5},{5,6},{6,7},{8,9},{9,10},{10,11},{12,13},{... | collective-permute-start | bytes 18440 | tf_op jit(solution)/shard_map/ppermute | solution.py:31
